TPU v7x, 256 devices: a whole 4x4x8 slice. The times are simulated.
256 devices in a mesh: owner: 16 (over z, core), tensor: 16 (over x, y).
Axes of the slice: x: 4, y: 4, z: 8, core: 2. Of those that a mesh axis runs over, the one named last changes fastest.
Arguments:
- mixer_input: bfloat16 [16384, 2, 8192], P('owner', None, 'tensor'), may hold values from -6 to 6
- step_raw: float32 [16384, 128], P('owner', 'tensor'), may hold values from -7 to 5
- decay_rate: float32 [128], P('tensor'), may hold values from 0.005 to 0.5
- skip_gain: float32 [128], P('tensor'), may hold values from 0.5 to 2
- state_proj: bfloat16 [16384, 2, 4, 256], P('owner'), may hold values from -1.5 to 1.5
- queries: bfloat16 [16384, 4096], P('owner', 'tensor'), may hold values from -256 to 256
- suffix_kv: bfloat16 [16384, 2, 4, 128], P('owner'), may hold values from -6 to 6
- state_pool: bfloat16 [64, 128, 64, 256], P('owner', 'tensor'), may hold values from -1.5 to 1.5
- page_pool: bfloat16 [256, 128, 2, 4, 128], P('owner'), may hold values from -6 to 6
- norm_gain: float32 [8192], P('tensor'), may hold values from 0.1 to 1.9
- hit_owner: int32 [64, 1], replicated, may hold values from 0 to 15; in each aligned block of 4 rows (0 to 3, 4 to 7, ...) at most 2 rows name the same one
- hit_slot: int32 [64], replicated, may hold values from 0 to 3
- page_owner: int32 [64, 16, 1], replicated, may hold values from 0 to 15; in each aligned block of 64 rows (0 to 63, 64 to 127, ..., all dimensions but the last counted through in order) at most 6 rows name the same one
- page_slot: int32 [64, 16], replicated, may hold values from 0 to 15
- prefix_len: int32 [64], replicated, may hold values from 256 to 2048, as said below
- suffix_len: int32 [64], replicated, may hold values from 64 to 256, as said below
Outputs:
- mamba_out: bfloat16 [16384, 8192], P('owner', 'tensor')
- attn_out: bfloat16 [16384, 4096], P('owner', 'tensor')
Inputs may be any that keep to these rules, and one draw needn't show every extreme that they name: `hit_owner`: the 4 requests on one index of owner name one owner at most 2 times, and some index reaches it. `page_owner`: of the 64 list entries of the requests on one index of owner, at most 6 name one owner, and some index reaches it. `prefix_len`: a multiple of 256; request 0 has 2048. `suffix_len`: request 0 has 256.
All inputs are finite; a program needn't handle non-finite values.
Results may differ from a plain program's by a relative error of at most 0.0045.
Values may be sent and summed in bfloat16 or wider, within the bound.
A program may use at most 192 MiB of HBM per device.

v0:
```python
import math
import jax
import jax.numpy as jnp
from jax import lax
from jax.sharding import PartitionSpec as P

SSM_HEAD_TOTAL = 128
MHDIM = 64
STATE = 256
GROUPS = 4
QHEADS = 32
KVHEADS = 4
HD = 128
PAGE = 128
SPAN = 128
SUF = 256
CAP_S = 2
MAXP = 16
EPSILON = 1e-05
NEG_FILL = -1e30


def mixer_core(x_heads, z_heads, rate_raw, decay_groups, skip_groups, b_rows, c_rows, start_state):
    seq_len, group_count, head_count, head_width = x_heads.shape
    blocks = seq_len // SPAN
    step_rate = jax.nn.softplus(rate_raw)
    keep_log = -step_rate * decay_groups[None]
    x_block = x_heads.reshape(blocks, SPAN, group_count, head_count, head_width)
    rate_block = step_rate.reshape(blocks, SPAN, group_count, head_count)
    cum_block = jnp.cumsum(keep_log.reshape(blocks, SPAN, group_count, head_count), axis=1)
    b_block = b_rows.reshape(blocks, SPAN, group_count, -1)
    c_block = c_rows.reshape(blocks, SPAN, group_count, -1)
    intersection = jnp.einsum(
        "cign,cjgn->cgij", c_block, b_block, preferred_element_type=jnp.float32
    )
    cum_moved = jnp.transpose(cum_block, (0, 2, 3, 1))
    rate_moved = jnp.transpose(rate_block, (0, 2, 3, 1))
    lower = jnp.arange(SPAN)[:, None] >= jnp.arange(SPAN)[None, :]
    fade = jnp.exp(jnp.where(lower, cum_moved[..., :, None] - cum_moved[..., None, :], NEG_FILL))
    weights = (intersection[:, :, None] * fade * rate_moved[..., None, :]).astype(jnp.bfloat16)
    inner = jnp.einsum("cghij,cjghp->cighp", weights, x_block, preferred_element_type=jnp.float32)
    cum_end = cum_block[:, -1]
    tail = jnp.exp(cum_end[:, None] - cum_block) * rate_block
    scaled = (tail[..., None] * x_block).astype(jnp.bfloat16)
    block_state = jnp.einsum(
        "cjghp,cjgn->cghpn", scaled, b_block, preferred_element_type=jnp.float32
    )
    carry = start_state.astype(jnp.float32)
    begins = []
    for block_index in range(blocks):
        begins.append(carry)
        carry = jnp.exp(cum_end[block_index])[..., None, None] * carry + block_state[block_index]
    begin_half = jnp.stack(begins).astype(jnp.bfloat16)
    carried = jnp.einsum(
        "cign,cghpn->cighp", c_block, begin_half, preferred_element_type=jnp.float32
    )
    summed = (
        inner
        + jnp.exp(cum_block)[..., None] * carried
        + skip_groups[None, None, :, :, None] * x_block
    )
    gate = jax.nn.silu(z_heads.astype(jnp.float32)).reshape(
        blocks, SPAN, group_count, head_count, head_width
    )
    return (summed * gate).reshape(seq_len, group_count, head_count, head_width)


def attend(query, key_pre, value_pre, key_suf, value_suf, prefix_count):
    softmax_scale = 1.0 / math.sqrt(HD)
    score_pre = (
        jnp.einsum("qhd,md->hqm", query, key_pre, preferred_element_type=jnp.float32)
        * softmax_scale
    )
    score_suf = (
        jnp.einsum("qhd,kd->hqk", query, key_suf, preferred_element_type=jnp.float32)
        * softmax_scale
    )
    pre_live = jnp.arange(key_pre.shape[0]) < prefix_count
    causal = jnp.arange(SUF)[:, None] >= jnp.arange(SUF)[None, :]
    score_pre = jnp.where(pre_live[None, None, :], score_pre, NEG_FILL)
    score_suf = jnp.where(causal[None], score_suf, NEG_FILL)
    row_max = jnp.maximum(jnp.max(score_pre, axis=2), jnp.max(score_suf, axis=2))
    weight_pre = jnp.exp(score_pre - row_max[..., None])
    weight_suf = jnp.exp(score_suf - row_max[..., None])
    denominator = jnp.sum(weight_pre, axis=2) + jnp.sum(weight_suf, axis=2)
    mixed = jnp.einsum(
        "hqm,md->qhd",
        weight_pre.astype(jnp.bfloat16),
        value_pre,
        preferred_element_type=jnp.float32,
    )
    mixed = mixed + jnp.einsum(
        "hqk,kd->qhd",
        weight_suf.astype(jnp.bfloat16),
        value_suf,
        preferred_element_type=jnp.float32,
    )
    return mixed / jnp.transpose(denominator)[:, :, None]


def bucket_plan(owner_rows, live_rows, owner_index, capacity):
    positions = jnp.arange(owner_rows.shape[1])
    matches = (
        (owner_rows[:, :, None] == owner_rows[:, None, :])
        & live_rows[:, None, :]
        & (positions[None, None, :] < positions[None, :, None])
    )
    slot_rank = jnp.sum(matches.astype(jnp.int32), axis=2)
    chosen = (
        (owner_rows[:, None, :] == owner_index)
        & live_rows[:, None, :]
        & (slot_rank[:, None, :] == jnp.arange(capacity)[None, :, None])
    )
    return (slot_rank, chosen)


def bucket_send(table, entry_ids, chosen):
    wanted = jnp.sum(jnp.where(chosen, entry_ids[:, None, :], 0), axis=2).reshape(-1)
    filled = jnp.any(chosen, axis=2).reshape(-1)
    picked = jnp.take(table, wanted, axis=0, mode="clip")
    shaped = jnp.where(
        filled.reshape((-1,) + (1,) * (picked.ndim - 1)), picked, jnp.zeros_like(picked)
    )
    return shaped.reshape(chosen.shape[:2] + picked.shape[1:])


def body(
    mixer_input,
    step_raw,
    decay_rate,
    skip_gain,
    state_proj,
    queries,
    suffix_kv,
    state_pool,
    page_pool,
    norm_gain,
    hit_owner,
    hit_slot,
    page_owner,
    page_slot,
    prefix_len,
    suffix_len,
):
    owners = lax.axis_size("owner")
    owner_index = lax.axis_index("owner")
    column = lax.axis_index("tensor")
    local_count = mixer_input.shape[0] // SUF
    local_heads = decay_rate.shape[0]
    local_qheads = queries.shape[1] // HD
    group_index = column * local_heads // (SSM_HEAD_TOTAL // GROUPS)
    kv_index = column * local_qheads // (QHEADS // KVHEADS)
    first_row = owner_index * local_count
    page_capacity = max(2, (local_count * MAXP + owners - 1) // owners * 3 // 2)
    state_owner = hit_owner[:, 0].reshape(owners, local_count)
    state_slot = hit_slot.reshape(owners, local_count)
    every_live = jnp.ones(state_owner.shape, jnp.bool_)
    state_rank, state_pick = bucket_plan(state_owner, every_live, owner_index, CAP_S)
    outgoing = bucket_send(state_pool, state_slot, state_pick)
    arrived = lax.all_to_all(outgoing, "owner", split_axis=0, concat_axis=0, tiled=True)
    arrived = arrived.reshape((owners * CAP_S,) + arrived.shape[2:])
    local_holder = lax.dynamic_index_in_dim(state_owner, owner_index, 0, keepdims=False)
    my_rank = lax.dynamic_index_in_dim(state_rank, owner_index, 0, keepdims=False)
    start_state = jnp.take(arrived, local_holder * CAP_S + my_rank, axis=0, mode="clip")
    x_heads = mixer_input[:, 0].reshape(local_count, SUF, 1, local_heads, MHDIM)
    z_heads = mixer_input[:, 1].reshape(local_count, SUF, 1, local_heads, MHDIM)
    rate_raw = step_raw.reshape(local_count, SUF, 1, local_heads)
    maps_here = lax.dynamic_index_in_dim(state_proj, group_index, 2, keepdims=True)
    b_rows = maps_here[:, 0].reshape(local_count, SUF, 1, STATE)
    c_rows = maps_here[:, 1].reshape(local_count, SUF, 1, STATE)
    core = jax.vmap(mixer_core, in_axes=(0, 0, 0, None, None, 0, 0, 0))
    gated = core(
        x_heads,
        z_heads,
        rate_raw,
        decay_rate.reshape(1, local_heads),
        skip_gain.reshape(1, local_heads),
        b_rows,
        c_rows,
        start_state.reshape(local_count, 1, local_heads, MHDIM, STATE),
    )
    gated = gated.reshape(local_count * SUF, local_heads * MHDIM)
    partial_sum = jnp.sum(gated * gated, axis=1)
    spread = jnp.where(jnp.arange(GROUPS)[:, None] == group_index, partial_sum[None, :], 0.0)
    totals = lax.psum(spread, "tensor")
    square = lax.dynamic_index_in_dim(totals, group_index, 0, keepdims=False) / (
        SSM_HEAD_TOTAL // GROUPS * MHDIM
    )
    my_suffix = lax.dynamic_slice_in_dim(suffix_len, first_row, local_count, 0)
    active = (jnp.arange(SUF)[None, :] < my_suffix[:, None]).reshape(-1)
    rescaled_input = gated * lax.rsqrt(square + EPSILON)[:, None] * norm_gain[None, :]
    mamba_out = jnp.where(active[:, None], rescaled_input, 0.0).astype(jnp.bfloat16)
    pool_head = lax.dynamic_index_in_dim(page_pool, kv_index, 3, keepdims=False)
    entries = local_count * MAXP
    page_rows = page_owner[:, :, 0].reshape(owners, entries)
    page_ids = page_slot.reshape(owners, entries)
    live_rows = (jnp.arange(MAXP)[None, :] * PAGE < prefix_len[:, None]).reshape(owners, entries)
    my_pages = lax.dynamic_index_in_dim(page_rows, owner_index, 0, keepdims=False)
    my_live = lax.dynamic_index_in_dim(live_rows, owner_index, 0, keepdims=False)
    page_rank, page_pick = bucket_plan(page_rows, live_rows, owner_index, page_capacity)
    sending = bucket_send(pool_head, page_ids, page_pick)
    received_rows = lax.all_to_all(sending, "owner", split_axis=0, concat_axis=0, tiled=True)
    received_rows = received_rows.reshape((owners * page_capacity,) + received_rows.shape[2:])
    my_page_rank = lax.dynamic_index_in_dim(page_rank, owner_index, 0, keepdims=False)
    fetched = jnp.take(received_rows, my_pages * page_capacity + my_page_rank, axis=0, mode="clip")
    fetched = jnp.where(my_live[:, None, None, None], fetched, jnp.zeros_like(fetched))
    prefix_kv = fetched.reshape(local_count, MAXP * PAGE, 2, HD)
    my_prefix = lax.dynamic_slice_in_dim(prefix_len, first_row, local_count, 0)
    owned_key_value = lax.dynamic_index_in_dim(suffix_kv, kv_index, 2, keepdims=False).reshape(
        local_count, SUF, 2, HD
    )
    query = queries.reshape(local_count, SUF, local_qheads, HD)
    mixed = jax.vmap(attend)(
        query,
        prefix_kv[:, :, 0],
        prefix_kv[:, :, 1],
        owned_key_value[:, :, 0],
        owned_key_value[:, :, 1],
        my_prefix,
    )
    attn_rows = mixed.reshape(local_count * SUF, local_qheads * HD)
    attn_out = jnp.where(active[:, None], attn_rows, 0.0).astype(jnp.bfloat16)
    return (mamba_out, attn_out)


def solution(mesh):
    return jax.shard_map(
        body,
        mesh=mesh,
        in_specs=(
            P("owner", None, "tensor"),
            P("owner", "tensor"),
            P("tensor"),
            P("tensor"),
            P("owner", None, None, None),
            P("owner", "tensor"),
            P("owner", None, None, None),
            P("owner", "tensor", None, None),
            P("owner", None, None, None, None),
            P("tensor"),
            P(),
            P(),
            P(),
            P(),
            P(),
            P(),
        ),
        out_specs=(P("owner", "tensor"), P("owner", "tensor")),
        check_vma=False,
    )
```

profile of v0, /device:TPU:96, one launch (start us, length us, event | category | flops | bytes accessed | tf_op | source)
XLA Modules:
  0.0 448.7 jit_solution(13598574537655978479)
XLA Ops:
  0.7 0.9 copy.186
  1.7 0.7 lt.143
  2.7 4.6 %constant_dynamic-slice_fusion.4 = bf16[16,128,2,1,128]{4,3,2,1,0:T(2,128)(2,1)S(1)} fusion(bf16[16,128,2,4,128]{4,3,2,1,0:T(4,128)(2,1)} %param.24, s32[]{:T(128)S(6)} %select_n.125), kind=kLoop, calls=%fused_computation.95 | loop fusion | bytes 2097156 | tf_op jit(solution)/shard_map/jit(dynamic_index_in_dim)/dynamic_slice | solution.py:193
  7.3 0.3 copy.249
  7.6 0.4 copy-done.11
  8.2 0.5 convert_reduce_fusion
  8.7 0.2 fusion.36
  8.9 0.2 select_reduce_fusion
  9.3 0.1 copy.187
  9.4 6.0 %gather_fusion.2 = bf16[96,128,2,128]{3,1,2,0:T(8,128)(2,1)} fusion(bf16[16,128,2,128]{3,1,2,0:T(8,128)(2,1)S(1)} %bitcast.137, s32[1024]{0:T(1024)S(1)} %pad_clamp_fusion.1), kind=kCustom, calls=%fused_computation.2 | custom fusion | bytes 12583296 | tf_op jit(solution)/shard_map/jit(_take)/gather | solution.py:120
  15.4 5.9 %broadcast_select_fusion.1 = bf16[16,6,128,2,128]{4,2,3,1,0:T(8,128)(2,1)} fusion(bf16[16,6,128,2,128]{4,2,3,1,0:T(8,128)(2,1)} %bitcast.139, pred[16,6]{1,0:T(8,128)(4,1)S(1)} %copy.187), kind=kLoop, calls=%fused_computation.13 | loop fusion | flops 3145728 | bytes 12583008 | tf_op jit(solution)/shard_map/jit(_where)/select_n | solution.py:121
  21.3 7.8 %all-to-all-start.1 = ((bf16[16,6,128,2,128]{4,2,3,1,0:T(8,128)(2,1)}), bf16[16,6,128,2,128]{4,2,3,1,0:T(8,128)(2,1)}, u32[]{:S(2)}, u32[]{:S(2)}) async-start(bf16[16,6,128,2,128]{4,2,3,1,0:T(8,128)(2,1)} %broadcast_select_fusion.1), calls=%async_computation.1 | async-start | bytes 12582912 | tf_op jit(solution)/shard_map/all_to_all | solution.py:202
  29.2 0.5 broadcast.269
  29.8 0.7 reduce.10
  30.7 0.1 convert_reduce_fusion.1
  31.0 0.1 copy.171
  31.2 4.8 %gather_fusion = bf16[32,8,64,256]{3,2,1,0:T(8,128)(2,1)} fusion(bf16[4,8,64,256]{3,2,1,0:T(8,128)(2,1)S(1)} %copy-done.2, s32[1024]{0:T(1024)S(1)} %pad_clamp_fusion.3), kind=kCustom, calls=%fused_computation | custom fusion | bytes 16777344 | tf_op jit(solution)/shard_map/jit(_take)/gather | solution.py:120
  36.0 7.2 %broadcast_select_fusion = bf16[16,2,8,64,256]{4,3,2,1,0:T(8,128)(2,1)} fusion(bf16[16,2,8,64,256]{4,3,2,1,0:T(8,128)(2,1)} %bitcast.138, pred[16,2]{1,0:T(8,128)(4,1)S(1)} %copy.171), kind=kLoop, calls=%fused_computation.12 | loop fusion | flops 4194304 | bytes 16777248 | tf_op jit(solution)/shard_map/jit(_where)/select_n | solution.py:121
  43.2 124.6 %all-to-all-done.1 = bf16[16,6,128,2,128]{4,2,3,1,0:T(8,128)(2,1)} async-done(((bf16[16,6,128,2,128]{4,2,3,1,0:T(8,128)(2,1)}), bf16[16,6,128,2,128]{4,2,3,1,0:T(8,128)(2,1)}, u32[]{:S(2)}, u32[]{:S(2)}) %all-to-all-start.1) | async-done | bytes 6291488 | tf_op jit(solution)/shard_map/all_to_all | solution.py:202
  167.8 5.3 %all-to-all-start = ((bf16[16,2,8,64,256]{4,3,2,1,0:T(8,128)(2,1)}), bf16[16,2,8,64,256]{4,3,2,1,0:T(8,128)(2,1)}, u32[]{:S(2)}, u32[]{:S(2)}) async-start(bf16[16,2,8,64,256]{4,3,2,1,0:T(8,128)(2,1)} %broadcast_select_fusion), calls=%async_computation | async-start | bytes 16777216 | tf_op jit(solution)/shard_map/all_to_all | solution.py:160
  173.1 6.9 %fusion.50 = (bf16[1024,1,512]{2,1,0:T(2,128)(2,1)}, bf16[1024,1,512]{2,1,0:T(2,128)(2,1)}) fusion(bf16[1024,2,512]{2,1,0:T(2,128)(2,1)} %param.16), kind=kLoop, calls=%fused_computation.115 | loop fusion | bytes 4194304 | tf_op jit(solution)/shard_map/slice | solution.py:166
  180.1 5.8 %copy.165 = bf16[1024,1,512]{0,2,1:T(8,128)(2,1)} copy(bf16[1024,1,512]{2,1,0:T(2,128)(2,1)} %get-tuple-element.15) | data formatting | bytes 2097152 | tf_op jit(solution)/shard_map/slice | solution.py:165
  185.9 4.7 %copy_convert_fusion = (f32[1024,1,512]{2,0,1:T(8,128)}, f32[1024,1,512]{2,0,1:T(8,128)}) fusion(bf16[1024,1,512]{2,1,0:T(2,128)(2,1)} %get-tuple-element.14, bf16[1024,1,512]{2,1,0:T(2,128)(2,1)} %get-tuple-element.15), kind=kLoop, calls=%fused_computation.52 | loop fusion | flops 1048576 | bytes 6291456 | tf_op jit(solution)/shard_map/vmap()/convert_element_type | solution.py:62
  190.7 6.1 %copy.182 = f32[1024,1,512]{0,1,2:T(1,128)} copy(f32[1024,1,512]{2,0,1:T(8,128)} %get-tuple-element.26) | data formatting | bytes 4194304 | tf_op jit(solution)/shard_map/vmap()/convert_element_type | solution.py:62
  196.8 6.1 %copy.179 = f32[1024,1,512]{0,1,2:T(1,128)} copy(f32[1024,1,512]{2,0,1:T(8,128)} %get-tuple-element.27) | data formatting | bytes 4194304 | tf_op jit(solution)/shard_map/vmap()/convert_element_type | solution.py:44
  202.9 5.4 %constant_dynamic-slice_fusion.8 = (bf16[1024,1,1,256]{3,2,1,0:T(2,128)(2,1)}, bf16[1024,1,1,256]{3,2,1,0:T(2,128)(2,1)S(1)}) fusion(bf16[1024,2,4,256]{3,2,1,0:T(4,128)(2,1)} %param.20, s32[]{:T(128)S(6)} %select_n.115, s32[]{:T(128)S(6)} %add.163), kind=kLoop, calls=%fused_computation.99 | loop fusion | bytes 2097160 | tf_op jit(solution)/shard_map/slice | solution.py:169
  208.3 1.0 copy.175
  209.4 1.0 copy.161
  210.4 1.4 fusion.53
  211.9 2.4 fusion.51
  214.3 1.2 copy.167
  215.5 0.2 copy.162
  215.6 1.3 copy.215
  217.0 2.6 reshape.579
  219.6 1.2 copy.176
  221.0 2.0 reshape.584
  223.2 1.1 constant_dynamic-slice_fusion.1
  224.4 0.2 fusion.42
  224.7 0.8 multiply_convert_fusion.2
  225.6 2.7 convolution_bitcast_fusion
  228.3 0.3 fusion.54
  228.6 0.5 fusion.52
  229.1 3.3 fusion.6
  232.5 5.9 %gather_fusion.3 = bf16[64,128,2,128]{3,1,2,0:T(8,128)(2,1)} fusion(bf16[96,128,2,128]{3,1,2,0:T(8,128)(2,1)} %bitcast.33, s32[1024]{0:T(1024)S(1)} %pad_clamp_fusion), kind=kCustom, calls=%fused_computation.3 | custom fusion | bytes 8388864 | tf_op jit(solution)/shard_map/jit(_take)/gather | solution.py:205
  238.5 2.5 copy.191
  241.0 2.1 bitcast_select_fusion
  243.1 3.2 bitcast_reduce_fusion
  246.3 0.3 fusion.21
  246.6 4.5 %fusion.1 = f32[4,2,256]{2,1,0:T(2,128)S(1)} fusion(f32[4,2048,256,2]{2,1,3,0:T(8,128)S(1)} %get-tuple-element.23, f32[4,2,256]{2,1,0:T(2,128)S(1)} %max.43, pred[4,2048]{1,0:T(4,128)(4,1)S(1)} %iota_compare_fusion.3), kind=kLoop, calls=%fused_computation.8 | loop fusion | flops 16775168 | bytes 16801792 | tf_op jit(solution)/shard_map/vmap()/reduce_sum | solution.py:85
  251.2 4.7 %fusion.3 = f32[4,128,2,256]{3,1,2,0:T(8,128)S(1)} fusion(f32[4,2048,256,2]{2,1,3,0:T(8,128)S(1)} %get-tuple-element.23, f32[4,2,256]{2,1,0:T(2,128)S(1)} %max.43, pred[4,2048]{1,0:T(4,128)(4,1)S(1)} %iota_compare_fusion.3, bf16[4,2048,2,128]{3,1,0,2:T(8,128)(2,1)S(1)} %bitcast_select_fusion), kind=kOutput, calls=%fused_computation.10 | convolution fusion | flops 1090519040 | bytes 19939328 | tf_op jit(solution)/shard_map/vmap(hqm,md->qhd)/dot_general | solution.py:86
  255.9 1.3 fusion.26
  257.2 1.3 copy.199
  258.5 1.0 fusion.28
  259.5 97.2 %all-to-all-done = bf16[16,2,8,64,256]{4,3,2,1,0:T(8,128)(2,1)} async-done(((bf16[16,2,8,64,256]{4,3,2,1,0:T(8,128)(2,1)}), bf16[16,2,8,64,256]{4,3,2,1,0:T(8,128)(2,1)}, u32[]{:S(2)}, u32[]{:S(2)}) %all-to-all-start) | async-done | bytes 8388640 | tf_op jit(solution)/shard_map/all_to_all | solution.py:160
  356.8 4.0 gather_fusion.1
  360.8 2.0 fusion.9
  362.8 0.1 copy-done.4
  363.0 0.6 copy-done.5
  363.6 2.6 multiply_reduce_fusion
  366.2 1.6 copy.185
  367.8 2.7 reshape.582
  370.7 74.6 %psum.7 = f32[4,1024]{1,0:T(4,128)S(1)} all-reduce(f32[4,1024]{1,0:T(4,128)S(1)} %broadcast_select_fusion.2), channel_id=1, replica_groups=mesh['owner'=16,'tensor'=16] {'tensor'}, use_global_device_ids=true, to_apply=%region_5.6 | all-reduce | flops 4096 | bytes 32768 | tf_op jit(solution)/shard_map/psum | solution.py:185
  445.3 2.0 select_convert_fusion
  447.4 1.3 copy.200
  (84 shorter events, 2.4 us)
Async XLA Ops:
  0.6 222.6 %copy-start = (bf16[1024,2,4,128]{3,2,1,0:T(4,128)(2,1)S(1)}, bf16[1024,2,4,128]{3,2,1,0:T(4,128)(2,1)}, u32[]{:S(2)}) copy-start(bf16[1024,2,4,128]{3,2,1,0:T(4,128)(2,1)} %param.22) | copy-start | bytes 6291460
  7.3 0.7 copy-start.11
  21.3 7.8 %copy-start.14 = (s32[64]{0:T(128)S(1)}, s32[64]{0:T(128)}, u32[]{:S(2)}) copy-start(s32[64]{0:T(128)} %param.27) | copy-start | bytes 772
  21.3 8.5 %copy-start.16 = (s32[64,1]{0,1:T(1,128)S(1)}, s32[64,1]{0,1:T(1,128)}, u32[]{:S(2)}) copy-start(s32[64,1]{0,1:T(1,128)} %param.26) | copy-start | bytes 772
  21.3 9.9 %copy-start.2 = (bf16[4,8,64,256]{3,2,1,0:T(8,128)(2,1)S(1)}, bf16[4,8,64,256]{3,2,1,0:T(8,128)(2,1)}, u32[]{:S(2)}) copy-start(bf16[4,8,64,256]{3,2,1,0:T(8,128)(2,1)} %param.23) | copy-start | bytes 3145732
  21.3 146.5 %all-to-all-start.1 = ((bf16[16,6,128,2,128]{4,2,3,1,0:T(8,128)(2,1)}), bf16[16,6,128,2,128]{4,2,3,1,0:T(8,128)(2,1)}, u32[]{:S(2)}, u32[]{:S(2)}) async-start(bf16[16,6,128,2,128]{4,2,3,1,0:T(8,128)(2,1)} %broadcast_select_fusion.1), calls=%async_computation.1 | async-start | bytes 12582912 | tf_op jit(solution)/shard_map/all_to_all | solution.py:202
  167.8 189.0 %all-to-all-start = ((bf16[16,2,8,64,256]{4,3,2,1,0:T(8,128)(2,1)}), bf16[16,2,8,64,256]{4,3,2,1,0:T(8,128)(2,1)}, u32[]{:S(2)}, u32[]{:S(2)}) async-start(bf16[16,2,8,64,256]{4,3,2,1,0:T(8,128)(2,1)} %broadcast_select_fusion), calls=%async_computation | async-start | bytes 16777216 | tf_op jit(solution)/shard_map/all_to_all | solution.py:160
  202.9 5.5 %copy-start.10 = (f32[1024,8]{0,1:T(8,128)S(1)}, f32[1024,8]{0,1:T(8,128)}, u32[]{:S(2)}) copy-start(f32[1024,8]{0,1:T(8,128)} %param.17) | copy-start | bytes 98308
  208.2 1.1 copy-start.13
  215.6 5.1 %copy-start.15 = (s32[64]{0:T(128)S(1)}, s32[64]{0:T(128)}, u32[]{:S(2)}) copy-start(s32[64]{0:T(128)} %param.30) | copy-start | bytes 772
  215.6 5.2 %copy-start.17 = (s32[64]{0:T(128)S(1)}, s32[64]{0:T(128)}, u32[]{:S(2)}) copy-start(s32[64]{0:T(128)} %param.31) | copy-start | bytes 772
  223.1 1.6 copy-start.3
  224.4 4.2 copy-start.6
  225.5 3.1 copy-start.8
  241.0 2.1 copy-start.9
  251.2 4.8 %copy-start.7 = (bf16[1024,2,1,128]{3,0,1,2:T(8,128)(2,1)S(1)}, bf16[1024,2,1,128]{3,0,1,2:T(8,128)(2,1)}, u32[]{:S(2)}) copy-start(bf16[1024,2,1,128]{3,0,1,2:T(8,128)(2,1)} %copy-done.6) | copy-start | bytes 1572868
  360.8 2.2 copy-start.4
  360.8 2.8 copy-start.5
  360.8 2.8 copy-start.18
  367.8 77.5 %copy-start.12 = (f32[512]{0:T(512)S(1)}, f32[512]{0:T(512)}, u32[]{:S(2)}) copy-start(f32[512]{0:T(512)} %param.25) | copy-start | bytes 6148
  445.3 3.4 copy-start.1
where the time goes:
time: 450 us; the launch traced here: 449 us
  waiting for transfers between devices  222 us (49%)
  local copies, waits for them, and re-layouts  82.6 us (18%)
  blocking collectives  74.6 us (17%)
  other arithmetic  36.9 us (8%)
  matrix products  18.6 us (4%)
  starting transfers between devices  13.1 us (3%)
    all_to_all x1, waiting for transfers between devices, body(): lax.all_to_all(sending, 'owner', split_axis=0, concat_axis=0, tiled=True)  125 us
    all_to_all x1, waiting for transfers between devices, body(): lax.all_to_all(outgoing, 'owner', split_axis=0, concat_axis=0, tiled=True)  97.2 us
    psum x1, blocking collectives, body(): totals = lax.psum(spread, 'tensor')  74.6 us
    select_n x2, other arithmetic, bucket_send(): jnp.where(filled.reshape((-1,) + (1,) * (picked.ndim - 1)), picked, jnp.z...  13.1 us
    gather x2, local copies, waits for them, and re-layouts, bucket_send(): picked = jnp.take(table, wanted, axis=0, mode='clip')  10.8 us
  transfers between devices with their start and end apart: 2, of which 2 were waited for; matrix products, arithmetic and copies ran while one was open for 22% of the time, Pallas kernels for 0%

commit v1 on v0

--- a/solution.py
+++ b/solution.py
@@ -18,6 +18,14 @@
 MAXP = 16
 EPSILON = 1e-05
 NEG_FILL = -1e30
+
+
+def _link_hubs(patch):
+    wide_n = lax.axis_size("tensor")
+    v_now = patch
+    for q in [[(i0, i0 ^ rr) for i0 in range(wide_n)] for rr in (1, 2, 4, 8, 16) if rr < wide_n]:
+        v_now = v_now + lax.ppermute(v_now, axis_name="tensor", perm=q)
+    return v_now
 
 
 def mixer_core(x_heads, z_heads, rate_raw, decay_groups, skip_groups, b_rows, c_rows, start_state):
@@ -182,7 +190,7 @@
     gated = gated.reshape(local_count * SUF, local_heads * MHDIM)
     partial_sum = jnp.sum(gated * gated, axis=1)
     spread = jnp.where(jnp.arange(GROUPS)[:, None] == group_index, partial_sum[None, :], 0.0)
-    totals = lax.psum(spread, "tensor")
+    totals = _link_hubs(spread)
     square = lax.dynamic_index_in_dim(totals, group_index, 0, keepdims=False) / (
         SSM_HEAD_TOTAL // GROUPS * MHDIM
     )

time: 450 us -> 397 us (0.88)
  blocking collectives: 74.6 us -> 0 us
  starting transfers between devices: 13.1 us -> 22.6 us
  waiting for transfers between devices: 222 us -> 229 us
    psum x1 -> x0, blocking collectives: 74.6 us -> none  [body(): totals = lax.psum(spread, 'tensor')]
    ppermute x0 -> x4, starting transfers between devices: none -> 9.49 us  [_link_hubs(): v_now = v_now + lax.ppermute(v_now, axis_name='tensor', perm=q)]
    ppermute x0 -> x4, waiting for transfers between devices: none -> 5.26 us  [_link_hubs(): v_now = v_now + lax.ppermute(v_now, axis_name='tensor', perm=q)]
  transfers between devices with their start and end apart: 2 -> 6, of which waited for: 2 -> 5; matrix products, arithmetic and copies ran while one was open for 22% -> 27% of each run, Pallas kernels for 0% -> 0%
where the time goes in v1:
time: 397 us; the launch traced here: 394 us
  waiting for transfers between devices  229 us (58%)
  local copies, waits for them, and re-layouts  83.3 us (21%)
  other arithmetic  37 us (9%)
  starting transfers between devices  22.6 us (6%)
  matrix products  20.9 us (5%)
    all_to_all x1, waiting for transfers between devices, body(): lax.all_to_all(sending, 'owner', split_axis=0, concat_axis=0, tiled=True)  125 us
    all_to_all x1, waiting for transfers between devices, body(): lax.all_to_all(outgoing, 'owner', split_axis=0, concat_axis=0, tiled=True)  99.2 us
    select_n x2, other arithmetic, bucket_send(): jnp.where(filled.reshape((-1,) + (1,) * (picked.ndim - 1)), picked, jnp.z...  13.1 us
    gather x2, local copies, waits for them, and re-layouts, bucket_send(): picked = jnp.take(table, wanted, axis=0, mode='clip')  10.8 us
    ppermute x4, starting transfers between devices, _link_hubs(): v_now = v_now + lax.ppermute(v_now, axis_name='tensor', perm=q)  9.49 us
    gather x2, local copies, waits for them, and re-layouts, body(): jnp.take(received_rows, my_pages * page_capacity + my_page_rank, axis=0,...  8.44 us
  transfers between devices with their start and end apart: 6, of which 5 were waited for; matrix products, arithmetic and copies ran while one was open for 27% of the time, Pallas kernels for 0%

profile of v1, /device:TPU:96, one launch (start us, length us, event | category | flops | bytes accessed | tf_op | source)
XLA Modules:
  0.0 393.9 jit_solution(2371737875186227969)
XLA Ops:
  0.7 0.9 copy.186
  1.7 0.7 lt.143
  2.7 4.6 %constant_dynamic-slice_fusion.4 = bf16[16,128,2,1,128]{4,3,2,1,0:T(2,128)(2,1)S(1)} fusion(bf16[16,128,2,4,128]{4,3,2,1,0:T(4,128)(2,1)} %param.24, s32[]{:T(128)S(6)} %select_n.125), kind=kLoop, calls=%fused_computation.97 | loop fusion | bytes 2097156 | tf_op jit(solution)/shard_map/jit(dynamic_index_in_dim)/dynamic_slice | solution.py:201
  7.3 0.3 copy.249
  7.6 0.4 copy-done.12
  8.2 0.5 convert_reduce_fusion
  8.9 0.2 select_reduce_fusion
  9.4 6.0 %gather_fusion.2 = bf16[96,128,2,128]{3,1,2,0:T(8,128)(2,1)} fusion(bf16[16,128,2,128]{3,1,2,0:T(8,128)(2,1)S(1)} %bitcast.137, s32[1024]{0:T(1024)S(1)} %pad_clamp_fusion.1), kind=kCustom, calls=%fused_computation.2 | custom fusion | bytes 12583296 | tf_op jit(solution)/shard_map/jit(_take)/gather | solution.py:128
  15.4 5.9 %broadcast_select_fusion.1 = bf16[16,6,128,2,128]{4,2,3,1,0:T(8,128)(2,1)} fusion(bf16[16,6,128,2,128]{4,2,3,1,0:T(8,128)(2,1)} %bitcast.139, pred[16,6]{1,0:T(8,128)(4,1)S(1)} %copy.187), kind=kLoop, calls=%fused_computation.13 | loop fusion | flops 3145728 | bytes 12583008 | tf_op jit(solution)/shard_map/jit(_where)/select_n | solution.py:129
  21.3 7.8 %all-to-all-start.1 = ((bf16[16,6,128,2,128]{4,2,3,1,0:T(8,128)(2,1)}), bf16[16,6,128,2,128]{4,2,3,1,0:T(8,128)(2,1)}, u32[]{:S(2)}, u32[]{:S(2)}) async-start(bf16[16,6,128,2,128]{4,2,3,1,0:T(8,128)(2,1)} %broadcast_select_fusion.1), calls=%async_computation.1 | async-start | bytes 12582912 | tf_op jit(solution)/shard_map/all_to_all | solution.py:210
  29.2 0.5 broadcast.269
  29.8 0.7 reduce.10
  31.2 4.8 %gather_fusion = bf16[32,8,64,256]{3,2,1,0:T(8,128)(2,1)} fusion(bf16[4,8,64,256]{3,2,1,0:T(8,128)(2,1)S(1)} %copy-done.2, s32[1024]{0:T(1024)S(1)} %pad_clamp_fusion.3), kind=kCustom, calls=%fused_computation | custom fusion | bytes 16777344 | tf_op jit(solution)/shard_map/jit(_take)/gather | solution.py:128
  36.0 7.2 %broadcast_select_fusion = bf16[16,2,8,64,256]{4,3,2,1,0:T(8,128)(2,1)} fusion(bf16[16,2,8,64,256]{4,3,2,1,0:T(8,128)(2,1)} %bitcast.138, pred[16,2]{1,0:T(8,128)(4,1)S(1)} %copy.171), kind=kLoop, calls=%fused_computation.12 | loop fusion | flops 4194304 | bytes 16777248 | tf_op jit(solution)/shard_map/jit(_where)/select_n | solution.py:129
  43.2 124.6 %all-to-all-done.1 = bf16[16,6,128,2,128]{4,2,3,1,0:T(8,128)(2,1)} async-done(((bf16[16,6,128,2,128]{4,2,3,1,0:T(8,128)(2,1)}), bf16[16,6,128,2,128]{4,2,3,1,0:T(8,128)(2,1)}, u32[]{:S(2)}, u32[]{:S(2)}) %all-to-all-start.1) | async-done | bytes 6291488 | tf_op jit(solution)/shard_map/all_to_all | solution.py:210
  167.8 5.3 %all-to-all-start = ((bf16[16,2,8,64,256]{4,3,2,1,0:T(8,128)(2,1)}), bf16[16,2,8,64,256]{4,3,2,1,0:T(8,128)(2,1)}, u32[]{:S(2)}, u32[]{:S(2)}) async-start(bf16[16,2,8,64,256]{4,3,2,1,0:T(8,128)(2,1)} %broadcast_select_fusion), calls=%async_computation | async-start | bytes 16777216 | tf_op jit(solution)/shard_map/all_to_all | solution.py:168
  173.1 6.9 %fusion.52 = (bf16[1024,1,512]{2,1,0:T(2,128)(2,1)}, bf16[1024,1,512]{2,1,0:T(2,128)(2,1)}) fusion(bf16[1024,2,512]{2,1,0:T(2,128)(2,1)} %param.16), kind=kLoop, calls=%fused_computation.118 | loop fusion | bytes 4194304 | tf_op jit(solution)/shard_map/slice | solution.py:174
  180.1 5.8 %copy.165 = bf16[1024,1,512]{0,2,1:T(8,128)(2,1)} copy(bf16[1024,1,512]{2,1,0:T(2,128)(2,1)} %get-tuple-element.15) | data formatting | bytes 2097152 | tf_op jit(solution)/shard_map/slice | solution.py:173
  185.9 4.7 %copy_convert_fusion = (f32[1024,1,512]{2,0,1:T(8,128)}, f32[1024,1,512]{2,0,1:T(8,128)}) fusion(bf16[1024,1,512]{2,1,0:T(2,128)(2,1)} %get-tuple-element.14, bf16[1024,1,512]{2,1,0:T(2,128)(2,1)} %get-tuple-element.15), kind=kLoop, calls=%fused_computation.52 | loop fusion | flops 1048576 | bytes 6291456 | tf_op jit(solution)/shard_map/vmap()/convert_element_type | solution.py:70
  190.7 6.1 %copy.182 = f32[1024,1,512]{0,1,2:T(1,128)} copy(f32[1024,1,512]{2,0,1:T(8,128)} %get-tuple-element.26) | data formatting | bytes 4194304 | tf_op jit(solution)/shard_map/vmap()/convert_element_type | solution.py:70
  196.8 6.1 %copy.179 = f32[1024,1,512]{0,1,2:T(1,128)} copy(f32[1024,1,512]{2,0,1:T(8,128)} %get-tuple-element.27) | data formatting | bytes 4194304 | tf_op jit(solution)/shard_map/vmap()/convert_element_type | solution.py:52
  202.9 5.4 %constant_dynamic-slice_fusion.8 = (bf16[1024,1,1,256]{3,2,1,0:T(2,128)(2,1)}, bf16[1024,1,1,256]{3,2,1,0:T(2,128)(2,1)S(1)}) fusion(bf16[1024,2,4,256]{3,2,1,0:T(4,128)(2,1)} %param.20, s32[]{:T(128)S(6)} %select_n.115, s32[]{:T(128)S(6)} %add.177), kind=kLoop, calls=%fused_computation.101 | loop fusion | bytes 2097160 | tf_op jit(solution)/shard_map/slice | solution.py:177
  208.3 1.0 copy.175
  209.4 1.0 copy.161
  210.4 1.4 fusion.55
  211.9 2.4 fusion.53
  214.3 1.2 copy.167
  215.6 1.3 copy.215
  217.0 2.6 reshape.579
  219.6 1.2 copy.176
  221.0 2.0 reshape.584
  223.2 1.1 constant_dynamic-slice_fusion.1
  224.4 0.2 fusion.43
  224.7 0.8 multiply_convert_fusion.2
  225.6 2.7 convolution_bitcast_fusion
  228.3 0.3 fusion.56
  228.6 1.8 fusion.54
  230.5 3.2 fusion.6
  233.8 5.9 %gather_fusion.3 = bf16[64,128,2,128]{3,1,2,0:T(8,128)(2,1)} fusion(bf16[96,128,2,128]{3,1,2,0:T(8,128)(2,1)} %bitcast.33, s32[1024]{0:T(1024)S(1)} %pad_clamp_fusion), kind=kCustom, calls=%fused_computation.3 | custom fusion | bytes 8388864 | tf_op jit(solution)/shard_map/jit(_take)/gather | solution.py:213
  239.7 2.5 copy.191
  242.3 2.1 bitcast_select_fusion
  244.4 3.2 bitcast_reduce_fusion
  247.6 4.5 %fusion.1 = f32[4,2,256]{2,1,0:T(2,128)S(1)} fusion(f32[4,2048,256,2]{2,1,3,0:T(8,128)S(1)} %get-tuple-element.23, f32[4,2,256]{2,1,0:T(2,128)S(1)} %max.43, pred[4,2048]{1,0:T(4,128)(4,1)S(1)} %iota_compare_fusion.3), kind=kLoop, calls=%fused_computation.8 | loop fusion | flops 16775168 | bytes 16801792 | tf_op jit(solution)/shard_map/vmap()/reduce_sum | solution.py:93
  252.1 5.5 %fusion.3 = f32[4,128,2,256]{3,1,2,0:T(8,128)} fusion(f32[4,2048,256,2]{2,1,3,0:T(8,128)S(1)} %get-tuple-element.23, f32[4,2,256]{2,1,0:T(2,128)S(1)} %max.43, pred[4,2048]{1,0:T(4,128)(4,1)S(1)} %iota_compare_fusion.3, bf16[4,2048,2,128]{3,1,0,2:T(8,128)(2,1)S(1)} %bitcast_select_fusion), kind=kOutput, calls=%fused_computation.10 | convolution fusion | flops 1090519040 | bytes 19939328 | tf_op jit(solution)/shard_map/vmap(hqm,md->qhd)/dot_general | solution.py:94
  257.6 99.2 %all-to-all-done = bf16[16,2,8,64,256]{4,3,2,1,0:T(8,128)(2,1)} async-done(((bf16[16,2,8,64,256]{4,3,2,1,0:T(8,128)(2,1)}), bf16[16,2,8,64,256]{4,3,2,1,0:T(8,128)(2,1)}, u32[]{:S(2)}, u32[]{:S(2)}) %all-to-all-start) | async-done | bytes 8388640 | tf_op jit(solution)/shard_map/all_to_all | solution.py:168
  356.8 4.0 %gather_fusion.1 = bf16[4,8,64,256]{3,2,1,0:T(8,128)(2,1)S(1)} fusion(bf16[32,8,64,256]{3,2,1,0:T(8,128)(2,1)} %bitcast.13, s32[1024]{0:T(1024)S(1)} %pad_clamp_fusion.2), kind=kCustom, calls=%fused_computation.1 | custom fusion | bytes 2097168 | tf_op jit(solution)/shard_map/jit(_take)/gather | solution.py:172
  360.8 2.0 fusion.9
  363.0 0.6 copy-done.5
  363.6 3.7 multiply_reduce_fusion
  367.4 1.6 collective-permute-start
  369.0 0.3 fusion.21
  369.3 1.9 collective-permute-done
  371.2 3.2 collective-permute-start.1
  374.4 2.0 collective-permute-done.1
  376.6 1.5 collective-permute-start.2
  378.1 0.5 fusion.26
  378.6 0.4 copy.199
  379.0 1.3 collective-permute-done.2
  380.3 3.2 collective-permute-start.3
  383.5 1.0 fusion.28
  384.5 3.2 copy.185
  387.7 2.7 reshape.582
  390.5 2.0 select_convert_fusion
  392.6 1.3 copy.200
  (98 shorter events, 3.4 us)
Async XLA Ops:
  0.6 222.6 %copy-start = (bf16[1024,2,4,128]{3,2,1,0:T(4,128)(2,1)S(1)}, bf16[1024,2,4,128]{3,2,1,0:T(4,128)(2,1)}, u32[]{:S(2)}) copy-start(bf16[1024,2,4,128]{3,2,1,0:T(4,128)(2,1)} %param.22) | copy-start | bytes 6291460
  7.3 0.7 copy-start.12
  21.3 7.8 %copy-start.15 = (s32[64]{0:T(128)S(1)}, s32[64]{0:T(128)}, u32[]{:S(2)}) copy-start(s32[64]{0:T(128)} %param.27) | copy-start | bytes 772
  21.3 8.5 %copy-start.17 = (s32[64,1]{0,1:T(1,128)S(1)}, s32[64,1]{0,1:T(1,128)}, u32[]{:S(2)}) copy-start(s32[64,1]{0,1:T(1,128)} %param.26) | copy-start | bytes 772
  21.3 9.9 %copy-start.2 = (bf16[4,8,64,256]{3,2,1,0:T(8,128)(2,1)S(1)}, bf16[4,8,64,256]{3,2,1,0:T(8,128)(2,1)}, u32[]{:S(2)}) copy-start(bf16[4,8,64,256]{3,2,1,0:T(8,128)(2,1)} %param.23) | copy-start | bytes 3145732
  21.3 146.5 %all-to-all-start.1 = ((bf16[16,6,128,2,128]{4,2,3,1,0:T(8,128)(2,1)}), bf16[16,6,128,2,128]{4,2,3,1,0:T(8,128)(2,1)}, u32[]{:S(2)}, u32[]{:S(2)}) async-start(bf16[16,6,128,2,128]{4,2,3,1,0:T(8,128)(2,1)} %broadcast_select_fusion.1), calls=%async_computation.1 | async-start | bytes 12582912 | tf_op jit(solution)/shard_map/all_to_all | solution.py:210
  167.8 189.0 %all-to-all-start = ((bf16[16,2,8,64,256]{4,3,2,1,0:T(8,128)(2,1)}), bf16[16,2,8,64,256]{4,3,2,1,0:T(8,128)(2,1)}, u32[]{:S(2)}, u32[]{:S(2)}) async-start(bf16[16,2,8,64,256]{4,3,2,1,0:T(8,128)(2,1)} %broadcast_select_fusion), calls=%async_computation | async-start | bytes 16777216 | tf_op jit(solution)/shard_map/all_to_all | solution.py:168
  202.9 5.5 %copy-start.11 = (f32[1024,8]{0,1:T(8,128)S(1)}, f32[1024,8]{0,1:T(8,128)}, u32[]{:S(2)}) copy-start(f32[1024,8]{0,1:T(8,128)} %param.17) | copy-start | bytes 98308
  208.2 1.1 copy-start.14
  215.6 5.1 %copy-start.16 = (s32[64]{0:T(128)S(1)}, s32[64]{0:T(128)}, u32[]{:S(2)}) copy-start(s32[64]{0:T(128)} %param.30) | copy-start | bytes 772
  215.6 5.2 %copy-start.18 = (s32[64]{0:T(128)S(1)}, s32[64]{0:T(128)}, u32[]{:S(2)}) copy-start(s32[64]{0:T(128)} %param.31) | copy-start | bytes 772
  223.1 1.6 copy-start.3
  224.4 4.2 %copy-start.7 = (bf16[1024,2,1,128]{3,0,1,2:T(8,128)(2,1)}, bf16[1024,2,1,128]{3,0,1,2:T(8,128)(2,1)S(1)}, u32[]{:S(2)}) copy-start(bf16[1024,2,1,128]{3,0,1,2:T(8,128)(2,1)S(1)} %copy.193) | copy-start | bytes 1572868
  225.5 3.1 copy-start.9
  242.2 2.1 copy-start.10
  360.8 2.2 copy-start.4
  360.8 2.8 copy-start.5
  360.8 2.8 copy-start.19
  363.6 5.4 %copy-start.6 = (f32[4,2,256,256]{2,3,1,0:T(8,128)S(1)}, f32[4,2,256,256]{2,3,1,0:T(8,128)}, u32[]{:S(2)}) copy-start(f32[4,2,256,256]{2,3,1,0:T(8,128)} %get-tuple-element.25) | copy-start | bytes 6291460
  367.3 10.8 %copy-start.8 = (bf16[1024,2,1,128]{3,0,1,2:T(8,128)(2,1)S(1)}, bf16[1024,2,1,128]{3,0,1,2:T(8,128)(2,1)}, u32[]{:S(2)}) copy-start(bf16[1024,2,1,128]{3,0,1,2:T(8,128)(2,1)} %copy-done.7) | copy-start | bytes 1572868
  367.3 10.8 %copy-start.20 = (f32[4,128,2,256]{3,1,2,0:T(8,128)S(1)}, f32[4,128,2,256]{3,1,2,0:T(8,128)}, u32[]{:S(2)}) copy-start(f32[4,128,2,256]{3,1,2,0:T(8,128)} %fusion.3) | copy-start | bytes 3145732
  367.4 3.8 collective-permute-start
  371.2 5.3 %collective-permute-start.1 = (f32[4,1024]{1,0:T(4,128)S(1)}, f32[4,1024]{1,0:T(4,128)S(1)}, u32[]{:S(2)}, u32[]{:S(2)}) collective-permute-start(f32[4,1024]{1,0:T(4,128)S(1)} %fusion.48), channel_id=1, source_target_pairs={{0,2},{1,3},{2,0},{3,1},{4,6},{5,7},{6,4},{7,5},{8,10},{9,11},{10,... | collective-permute-start | bytes 49160 | tf_op jit(solution)/shard_map/ppermute | solution.py:27
  376.6 3.8 collective-permute-start.2
  380.3 10.1 %collective-permute-start.3 = (f32[4,1024]{1,0:T(4,128)S(1)}, f32[4,1024]{1,0:T(4,128)S(1)}, u32[]{:S(2)}, u32[]{:S(2)}) collective-permute-start(f32[4,1024]{1,0:T(4,128)S(1)} %add.161), channel_id=1, source_target_pairs={{0,8},{1,9},{2,10},{3,11},{4,12},{5,13},{6,14},{7,15},{8,0},{9,1},... | collective-permute-start | bytes 49160 | tf_op jit(solution)/shard_map/ppermute | solution.py:27
  387.7 2.8 copy-start.13
  390.5 3.4 copy-start.1
